TPU v7x, 32 devices: a whole 2x2x4 slice. The times are simulated.
32 devices in a mesh: shard: 4 (over z), ctx: 4 (over x, core), tp: 2 (over y).
Axes of the slice: x: 2, y: 2, z: 4, core: 2. Of those that a mesh axis runs over, the one named last changes fastest.
Arguments:
- hidden_in: bfloat16 [4, 1024, 1024], P('shard', 'ctx'), may hold values from -6 to 6
- out_grad: bfloat16 [4, 1024, 1024], P('shard', 'ctx'), may hold values from -6 to 6
- segment_ids: int32 [4, 1024], P('shard'), may hold values from 0 to 3, never falling along the last dimension, each value on 1 to 512 neighbouring positions
- w_qkv: bfloat16 [3, 1024, 1024], P(None, 'shard', 'tp'), may hold values from -0.1875 to 0.1875
- bias_qv: float32 [2, 1024], P(None, 'tp'), may hold values from -3 to 3
- w_out: bfloat16 [1024, 1024], P('tp', 'shard'), may hold values from -0.75 to 0.75
- bias_out: float32 [1024], replicated, may hold values from -3 to 3
- norm1_gain: float32 [1024], replicated, may hold values from 0.5 to 1.5
- norm1_shift: float32 [1024], replicated, may hold values from -3 to 3
- w_up: bfloat16 [1024, 4096], P('shard', 'tp'), may hold values from -0.1875 to 0.1875
- bias_up: float32 [4096], P('tp'), may hold values from -3 to 3
- w_down: bfloat16 [4096, 1024], P('tp', 'shard'), may hold values from -0.09375 to 0.09375
- bias_down: float32 [1024], replicated, may hold values from -3 to 3
- norm2_gain: float32 [1024], replicated, may hold values from 0.5 to 1.5
- norm2_shift: float32 [1024], replicated, may hold values from -3 to 3
Outputs:
- output: bfloat16 [4, 1024, 1024], P('shard', 'ctx')
- input_grad: bfloat16 [4, 1024, 1024], P('shard', 'ctx')
- w_qkv_grad: float32 [3, 1024, 1024], P(None, 'shard', 'tp')
- bias_qv_grad: float32 [2, 1024], P(None, 'tp')
- w_out_grad: float32 [1024, 1024], P('tp', 'shard')
- bias_out_grad: float32 [1024], replicated
- norm1_gain_grad: float32 [1024], replicated
- norm1_shift_grad: float32 [1024], replicated
- w_up_grad: float32 [1024, 4096], P('shard', 'tp')
- bias_up_grad: float32 [4096], P('tp')
- w_down_grad: float32 [4096, 1024], P('tp', 'shard')
- bias_down_grad: float32 [1024], replicated
- norm2_gain_grad: float32 [1024], replicated
- norm2_shift_grad: float32 [1024], replicated
Inputs may be any that keep to these rules, and one draw needn't show every extreme that they name: `segment_ids`: within each sequence the ids never fall and start at 0; each document has at most 512 tokens, and some document has exactly that many.
All inputs are finite; a program needn't handle non-finite values.
Results may differ from a plain program's by a relative error of at most 0.022.
The roundings to bfloat16 on the way count: a program that leaves them out, or rounds other values in their place, can miss the bound.
Values may be sent and summed in bfloat16 or wider, within the bound.
A program may use at most 128 MiB of HBM per device.

v0:
```python
import math

import jax
import jax.numpy as jnp
from jax import lax
from jax.sharding import PartitionSpec as P

HEADS = 16


EPSILON = 1e-05


def normalize(resid, gain, shift):
    average = jnp.mean(resid, axis=-1, keepdims=True)
    centred = resid - average
    variance = jnp.mean(centred * centred, axis=-1, keepdims=True)
    inv_std = lax.rsqrt(variance + EPSILON)
    normed = centred * inv_std
    return (normed * gain + shift, normed, inv_std)


def normalize_back(cotan, normed, inv_std, gain):
    scaled = cotan * gain
    return inv_std * (
        scaled
        - jnp.mean(scaled, axis=-1, keepdims=True)
        - normed * jnp.mean(scaled * normed, axis=-1, keepdims=True)
    )


def gelu_value(pre_act):
    return 0.5 * pre_act * (1.0 + jax.scipy.special.erf(pre_act * 0.7071067811865476))


def gelu_slope(pre_act):
    return (
        0.5 * (1.0 + jax.scipy.special.erf(pre_act * 0.7071067811865476))
        + pre_act * jnp.exp(-0.5 * pre_act * pre_act) * 0.3989422804014327
    )


def block_scores(query_block, keys, ids_block, ids_whole, scale):
    scores = (
        jnp.einsum("qhe,khe->hqk", query_block, keys, preferred_element_type=jnp.float32) * scale
    )
    return jnp.where((ids_block[:, None] == ids_whole[None, :])[None], scores, -jnp.inf)


def shards(
    hidden_in,
    out_grad,
    segment_ids,
    w_qkv,
    bias_qv,
    w_out,
    bias_out,
    norm1_gain,
    norm1_shift,
    w_up,
    bias_up,
    w_down,
    bias_down,
    norm2_gain,
    norm2_shift,
):
    seq_count, local_len, width = hidden_in.shape
    ctx_count = lax.axis_size("ctx")
    full_len = local_len * ctx_count
    row_count = seq_count * local_len
    head_dim = width // HEADS
    scale = 1.0 / math.sqrt(head_dim)
    qkv_full, out_full, up_full, down_full = (
        lax.all_gather(w_qkv, "shard", axis=1, tiled=True),
        lax.all_gather(w_out, "shard", axis=1, tiled=True),
        lax.all_gather(w_up, "shard", axis=0, tiled=True),
        lax.all_gather(w_down, "shard", axis=1, tiled=True),
    )
    local_cols = qkv_full.shape[2]
    group_cols = local_cols // ctx_count
    local_heads = group_cols // head_dim
    block_rows = min(512, full_len)
    block_count = full_len // block_rows
    tokens = hidden_in.reshape(row_count, width)
    bias_three = jnp.stack([bias_qv[0], jnp.zeros_like(bias_qv[0]), bias_qv[1]])
    project = (
        jnp.einsum("td,kde->tke", tokens, qkv_full, preferred_element_type=jnp.float32)
        + bias_three[None]
    )
    project = project.astype(jnp.bfloat16).reshape(seq_count, local_len, 3, ctx_count, group_cols)
    heads = lax.all_to_all(project, "ctx", split_axis=3, concat_axis=1, tiled=True)
    heads = heads.reshape(seq_count, full_len, 3, local_heads, head_dim)

    def attend_sequence(packed):
        seq_heads, seq_ids = packed
        keys = seq_heads[:, 1]
        values = seq_heads[:, 2]
        queries = seq_heads[:, 0].reshape(block_count, block_rows, local_heads, head_dim)
        id_blocks = seq_ids.reshape(block_count, block_rows)

        def attend_block(piece):
            query_block, ids_block = piece
            scores = block_scores(query_block, keys, ids_block, seq_ids, scale)
            log_total = jax.nn.logsumexp(scores, axis=-1)
            probs_low = jnp.exp(scores - log_total[..., None]).astype(jnp.bfloat16)
            attended = jnp.einsum(
                "hqk,khe->qhe", probs_low, values, preferred_element_type=jnp.float32
            ).astype(jnp.bfloat16)
            return (attended, log_total)

        attended, log_total = lax.map(attend_block, (queries, id_blocks))
        return (attended.reshape(full_len, local_heads, head_dim), log_total)

    attended_heads, log_totals = lax.map(attend_sequence, (heads, segment_ids))
    attended_tok = lax.all_to_all(
        attended_heads.reshape(seq_count, full_len, 1, group_cols),
        "ctx",
        split_axis=1,
        concat_axis=2,
        tiled=True,
    )
    attended_tok = attended_tok.reshape(row_count, local_cols)
    attn_part = jnp.dot(attended_tok, out_full, preferred_element_type=jnp.float32)
    resid_one = (
        lax.psum(attn_part.astype(jnp.bfloat16), "tp").astype(jnp.float32)
        + bias_out
        + tokens.astype(jnp.float32)
    )
    first, normed_one, inv_one = normalize(resid_one, norm1_gain, norm1_shift)
    first_low = first.astype(jnp.bfloat16)
    pre_act = jnp.dot(first_low, up_full, preferred_element_type=jnp.float32) + bias_up
    activated = gelu_value(pre_act).astype(jnp.bfloat16)
    ffn_part = jnp.dot(activated, down_full, preferred_element_type=jnp.float32)
    resid_two = (
        lax.psum(ffn_part.astype(jnp.bfloat16), "tp").astype(jnp.float32) + bias_down + first
    )
    result, normed_two, inv_two = normalize(resid_two, norm2_gain, norm2_shift)
    grad_float = out_grad.reshape(row_count, width).astype(jnp.float32)
    gain_two_grad = jnp.sum(grad_float * normed_two, axis=0)
    shift_two_grad = jnp.sum(grad_float, axis=0)
    resid_two_grad = normalize_back(grad_float, normed_two, inv_two, norm2_gain)
    resid_two_low = resid_two_grad.astype(jnp.bfloat16)
    bias_down_grad = jnp.sum(resid_two_grad, axis=0)
    act_grad = jnp.dot(resid_two_low, down_full.T, preferred_element_type=jnp.float32)
    pre_grad = act_grad * gelu_slope(pre_act)
    pre_low = pre_grad.astype(jnp.bfloat16)
    bias_up_grad = jnp.sum(pre_grad, axis=0)
    back_part = jnp.dot(pre_low, up_full.T, preferred_element_type=jnp.float32)
    first_grad = resid_two_grad + lax.psum(back_part.astype(jnp.bfloat16), "tp").astype(jnp.float32)
    gain_one_grad = jnp.sum(first_grad * normed_one, axis=0)
    shift_one_grad = jnp.sum(first_grad, axis=0)
    resid_one_grad = normalize_back(first_grad, normed_one, inv_one, norm1_gain)
    resid_one_low = resid_one_grad.astype(jnp.bfloat16)
    bias_out_grad = jnp.sum(resid_one_grad, axis=0)
    attended_grad = jnp.dot(resid_one_low, out_full.T, preferred_element_type=jnp.float32).astype(
        jnp.bfloat16
    )
    grad_heads = lax.all_to_all(
        attended_grad.reshape(seq_count, local_len, ctx_count, group_cols),
        "ctx",
        split_axis=2,
        concat_axis=1,
        tiled=True,
    )
    grad_heads = grad_heads.reshape(seq_count, full_len, local_heads, head_dim)

    def back_sequence(packed):
        seq_heads, seq_ids, seq_attended, seq_grad, seq_log = packed
        keys = seq_heads[:, 1]
        values = seq_heads[:, 2]
        queries = seq_heads[:, 0].reshape(block_count, block_rows, local_heads, head_dim)
        id_blocks = seq_ids.reshape(block_count, block_rows)
        att_blocks = seq_attended.reshape(block_count, block_rows, local_heads, head_dim)
        grad_blocks = seq_grad.reshape(block_count, block_rows, local_heads, head_dim)

        def back_block(carry, piece):
            key_total, value_total = carry
            query_block, ids_block, att_block, grad_block, log_block = piece
            scores = block_scores(query_block, keys, ids_block, seq_ids, scale)
            probs = jnp.exp(scores - log_block[..., None])
            probs_low = probs.astype(jnp.bfloat16)
            prob_grad = jnp.einsum(
                "qhe,khe->hqk", grad_block, values, preferred_element_type=jnp.float32
            )
            offset = jnp.sum(
                grad_block.astype(jnp.float32) * att_block.astype(jnp.float32), axis=-1
            ).T
            score_grad = (probs * (prob_grad - offset[..., None]) * scale).astype(jnp.bfloat16)
            query_grad = jnp.einsum(
                "hqk,khe->qhe", score_grad, keys, preferred_element_type=jnp.float32
            ).astype(jnp.bfloat16)
            key_total = key_total + jnp.einsum(
                "hqk,qhe->khe", score_grad, query_block, preferred_element_type=jnp.float32
            )
            value_total = value_total + jnp.einsum(
                "hqk,qhe->khe", probs_low, grad_block, preferred_element_type=jnp.float32
            )
            return ((key_total, value_total), query_grad)

        empty = jnp.zeros((full_len, local_heads, head_dim), jnp.float32)
        (key_total, value_total), query_grads = lax.scan(
            back_block, (empty, empty), (queries, id_blocks, att_blocks, grad_blocks, seq_log)
        )
        return jnp.stack(
            [
                query_grads.reshape(full_len, local_heads, head_dim),
                key_total.astype(jnp.bfloat16),
                value_total.astype(jnp.bfloat16),
            ],
            axis=1,
        )

    head_grads = lax.map(
        back_sequence, (heads, segment_ids, attended_heads, grad_heads, log_totals)
    )
    proj_grad = lax.all_to_all(
        head_grads.reshape(seq_count, full_len, 3, 1, group_cols),
        "ctx",
        split_axis=1,
        concat_axis=3,
        tiled=True,
    )
    proj_grad = proj_grad.reshape(row_count, 3, local_cols)
    bias_qv_grad = jnp.stack(
        [
            jnp.sum(proj_grad[:, 0].astype(jnp.float32), axis=0),
            jnp.sum(proj_grad[:, 2].astype(jnp.float32), axis=0),
        ]
    )
    input_part = jnp.einsum("tke,kde->td", proj_grad, qkv_full, preferred_element_type=jnp.float32)
    input_grad = (
        resid_one_grad + lax.psum(input_part.astype(jnp.bfloat16), "tp").astype(jnp.float32)
    ).astype(jnp.bfloat16)
    shard_rows = width // lax.axis_size("shard")
    part_qkv = jnp.einsum(
        "td,tke->dke", tokens, proj_grad, preferred_element_type=jnp.float32
    ).reshape(shard_rows * lax.axis_size("shard"), 3 * local_cols)
    part_out = jnp.einsum(
        "td,te->de", resid_one_low, attended_tok, preferred_element_type=jnp.float32
    )
    part_up = jnp.einsum("td,te->de", first_low, pre_low, preferred_element_type=jnp.float32)
    part_down = jnp.einsum(
        "td,te->de", resid_two_low, activated, preferred_element_type=jnp.float32
    )
    owned = lax.psum_scatter(
        jnp.concatenate([part_qkv, part_out, part_up, part_down], axis=1).astype(jnp.bfloat16),
        "shard",
        scatter_dimension=0,
        tiled=True,
    ).astype(jnp.float32)
    owned = lax.psum(owned.astype(jnp.bfloat16), "ctx").astype(jnp.float32)
    owned_rows = owned.shape[0]
    hidden_cols = pre_low.shape[1]
    qkv_grad = owned[:, : 3 * local_cols].reshape(owned_rows, 3, local_cols).transpose(1, 0, 2)
    out_weight_grad = owned[:, 3 * local_cols : 4 * local_cols].T
    up_grad = owned[:, 4 * local_cols : 4 * local_cols + hidden_cols]
    down_grad = owned[:, 4 * local_cols + hidden_cols :].T
    small = lax.psum(
        (
            bias_qv_grad,
            bias_out_grad,
            gain_one_grad,
            shift_one_grad,
            bias_up_grad,
            bias_down_grad,
            gain_two_grad,
            shift_two_grad,
        ),
        ("shard", "ctx"),
    )
    output = result.astype(jnp.bfloat16).reshape(seq_count, local_len, width)
    return (
        output,
        input_grad.reshape(seq_count, local_len, width),
        qkv_grad,
        small[0],
        out_weight_grad,
        small[1],
        small[2],
        small[3],
        up_grad,
        small[4],
        down_grad,
        small[5],
        small[6],
        small[7],
    )


def solution(mesh):
    return jax.shard_map(
        shards,
        mesh=mesh,
        in_specs=(
            P("shard", "ctx", None),
            P("shard", "ctx", None),
            P("shard", None),
            P(None, "shard", "tp"),
            P(None, "tp"),
            P("tp", "shard"),
            P(),
            P(),
            P(),
            P("shard", "tp"),
            P("tp"),
            P("tp", "shard"),
            P(),
            P(),
            P(),
        ),
        out_specs=(
            P("shard", "ctx", None),
            P("shard", "ctx", None),
            P(None, "shard", "tp"),
            P(None, "tp"),
            P("tp", "shard"),
            P(),
            P(),
            P(),
            P("shard", "tp"),
            P("tp"),
            P("tp", "shard"),
            P(),
            P(),
            P(),
        ),
        check_vma=False,
    )
```

profile of v0, /device:TPU:0, one launch (start us, length us, event | category | flops | bytes accessed | tf_op | source)
XLA Modules:
  0.0 789.5 jit_solution(12445965865894515886)
XLA Ops:
  8.8 66.9 %all-gather.5.cloned.1.call-done = bf16[3,1024,512]{2,1,0:T(8,128)(2,1)} async-done(((bf16[3,256,512]{2,1,0:T(8,128)(2,1)}), bf16[3,1024,512]{2,1,0:T(8,128)(2,1)}) %all-gather.5.cloned.1.call-update) | async-done | bytes 3145744 | tf_op jit(solution)/shard_map/all_gather | solution.py:74
  80.0 3.5 all-to-all-start
  85.5 9.6 %all-to-all-done = bf16[1,256,3,4,128]{4,1,2,0,3:T(8,128)(2,1)S(1)} async-done(((bf16[1,256,3,4,128]{4,1,2,0,3:T(8,128)(2,1)}), bf16[1,256,3,4,128]{4,1,2,0,3:T(8,128)(2,1)S(1)}, u32[]{:S(2)}, u32[]{:S(2)}) %all-to-all-start) | async-done | bytes 786464 | tf_op jit(solution)/shard_map/all_to_all | solution.py:91
  96.7 7.9 %while.45 = (s32[]{:T(128)}, bf16[2,512,2,64]{1,3,2,0:T(8,128)(2,1)S(1)}, f32[2,2,512]{2,1,0:T(2,128)S(1)}, s32[2,512]{1,0:T(2,128)S(1)}, s32[1024]{0:T(1024)S(1...) while((s32[]{:T(128)}, ...), condition=%wide.region_3.4_spmd, body=%wide.region_0.3_spmd.sunk | while | flops 280567808 | bytes 15526005 | solution.py:111
  108.2 8.4 %all_to_all.60 = bf16[4,2,16384]{2,1,0:T(2,128)(2,1)S(1)} all-to-all(bf16[4,2,16384]{2,1,0:T(2,128)(2,1)S(1)} %reshape.279), channel_id=1, replica_groups=mesh['shard'=4,'ctx'=4,'tp'=2] {'ctx'}, dimensions={0} | all-to-all | bytes 524288 | tf_op jit(solution)/shard_map/all_to_all | solution.py:115
  121.1 25.2 %all-reduce.7.cloned.1.call-done = bf16[256,1024]{1,0:T(8,128)(2,1)} async-done(((bf16[256,1024]{1,0:T(8,128)(2,1)}), bf16[256,1024]{1,0:T(8,128)(2,1)}) %all-reduce.7.cloned.1.call-update) | async-done | bytes 524304 | tf_op jit(solution)/shard_map/psum | solution.py:125
  149.0 79.5 %all-gather.9.cloned.1.call-done = bf16[1024,2048]{1,0:T(8,128)(2,1)} async-done(((bf16[256,2048]{1,0:T(8,128)(2,1)}), bf16[1024,2048]{1,0:T(8,128)(2,1)}) %all-gather.9.cloned.1.call-update) | async-done | bytes 4194320 | tf_op jit(solution)/shard_map/all_gather | solution.py:76
  228.5 5.6 multiply_convert_fusion.1
  234.1 74.8 %all-gather.11.cloned.1.call-done = bf16[2048,1024]{1,0:T(8,128)(2,1)} async-done(((bf16[2048,256]{1,0:T(8,128)(2,1)}), bf16[2048,1024]{1,0:T(8,128)(2,1)}) %all-gather.11.cloned.1.call-update) | async-done | bytes 4194320 | tf_op jit(solution)/shard_map/all_gather | solution.py:77
  309.0 4.6 convolution_convert_fusion.7
  313.6 26.9 %all-reduce.9.cloned.1.call-done = bf16[256,1024]{1,0:T(8,128)(2,1)} async-done(((bf16[256,1024]{1,0:T(8,128)(2,1)}), bf16[256,1024]{1,0:T(8,128)(2,1)}) %all-reduce.9.cloned.1.call-update) | async-done | bytes 524304 | tf_op jit(solution)/shard_map/psum | solution.py:135
  349.7 28.8 %all-reduce.11.cloned.1.call-done = bf16[256,1024]{1,0:T(8,128)(2,1)} async-done(((bf16[256,1024]{1,0:T(8,128)(2,1)}), bf16[256,1024]{1,0:T(8,128)(2,1)}) %all-reduce.11.cloned.1.call-update) | async-done | bytes 524304 | tf_op jit(solution)/shard_map/psum | solution.py:149
  385.9 4.3 all-to-all-start.2
  390.1 4.6 convolution_convert_fusion.2
  397.4 12.0 %while.46 = (s32[]{:T(128)}, f32[1024,2,64]{0,2,1:T(8,128)S(1)}, f32[1024,2,64]{0,2,1:T(8,128)}, bf16[2,512,2,64]{1,3,2,0:T(8,128)(2,1)S(1)}, bf16[2,512,2,64]{1...) while((s32[]{:T(128)}, f32[1024,2,64]{0,2,1:T(8,128)S(1)}, ...), condition=%wide.region_17.18_spmd.clone, body=%wide.region_15.17_spmd.clone.sunk | while | flops 683998208 | bytes 29526284 | solution.py:201
  412.4 4.2 all-to-all-start.3
  416.8 4.5 convolution_convert_fusion.1
  423.1 8.1 %all-to-all-done.3 = bf16[1,1024,3,1,128]{4,2,3,0,1:T(4,128)(2,1)} async-done(((bf16[1,1024,3,1,128]{4,2,3,0,1:T(4,128)(2,1)}), bf16[1,1024,3,1,128]{4,2,3,0,1:T(4,128)(2,1)}, u32[]{:S(2)}, u32[]{:S(2)}) %all-to-all-start.3) | async-done | bytes 786464 | tf_op jit(solution)/shard_map/all_to_all | solution.py:216
  438.4 4.6 copy.110
  443.0 10.9 %pad_maximum_fusion = bf16[1024,6144]{1,0:T(8,128)(2,1)} fusion(bf16[1024,2048]{1,0:T(8,128)(2,1)} %convolution_convert_fusion.1, bf16[1024,2048]{1,0:T(8,128)(2,1)} %convolution_convert_fusion.2, bf16[1024,512]{1,0:T(8,128)(2,1)} %copy.111, bf16[1024,1536]{1,0:T(8,128)(2,1)} %copy.110), kind=kLoop, calls=%fused_computation.55 | loop fusion | flops 50331648 | bytes 25165824 | tf_op jit(solution)/shard_map/concatenate | solution.py:246
  454.2 3.7 fusion.53
  458.0 207.0 %reduce-scatter.2.cloned.1.call-done = bf16[256,6144]{1,0:T(8,128)(2,1)} async-done(((bf16[1024,6144]{1,0:T(8,128)(2,1)}), bf16[256,6144]{1,0:T(8,128)(2,1)}) %reduce-scatter.2.cloned.1.call-update) | async-done | bytes 3145744 | tf_op jit(solution)/shard_map/reduce_scatter | solution.py:245
  665.3 62.3 %all-reduce = (f32[2,512]{1,0:T(2,128)}, f32[1024]{0:T(1024)}, f32[1024]{0:T(1024)}, f32[1024]{0:T(1024)}, f32[2048]{0:T(1024)}, /*index=5*/f32[1024]{0:T(1024)}, f32[1024]{0:T(1024)}, f32[1024]{0:T(1024)}) all-reduce(f32[2,512]{1,0:T(2,128)S(1)} %pad_maximum_fusion.3, ...), channel_id=1, replica_groups=mesh['shard'=4,'ctx'=4,'tp'=2] {'shard','ctx'}, use_global_device_ids=true, to_apply=%region_23.24 | all-reduce | flops 9216 | bytes 73728 | tf_op jit(solution)/shard_map/psum | solution.py:258
  729.6 39.1 %all-reduce.15.cloned.1.call-done = bf16[256,6144]{1,0:T(8,128)(2,1)} async-done(((bf16[256,6144]{1,0:T(8,128)(2,1)}), bf16[256,6144]{1,0:T(8,128)(2,1)}) %all-reduce.15.cloned.1.call-update) | async-done | bytes 3145744 | tf_op jit(solution)/shard_map/psum | solution.py:251
  (192 shorter events, 87.2 us)
Async XLA Ops:
  7.2 68.6 %all-gather.5.cloned.1.call-start = ((), (), s32[]{:S(2)}) async-start(), calls=%async_computation.5 | async-start | bytes 3932160 | tf_op jit(solution)/shard_map/all_gather | solution.py:74
  8.8 76.0 %copy-start.14 = (s32[1,1024]{1,0:T(1,128)S(1)}, s32[1,1024]{1,0:T(1,128)}, u32[]{:S(2)}) copy-start(s32[1,1024]{1,0:T(1,128)} %param.21) | copy-start | bytes 12292
  80.0 15.1 %all-to-all-start = ((bf16[1,256,3,4,128]{4,1,2,0,3:T(8,128)(2,1)}), bf16[1,256,3,4,128]{4,1,2,0,3:T(8,128)(2,1)S(1)}, u32[]{:S(2)}, u32[]{:S(2)}) async-start(bf16[1,256,3,4,128]{4,1,2,0,3:T(8,128)(2,1)} %copy.95), calls=%async_computation | async-start | bytes 1572864 | tf_op jit(solution)/shard_map/all_to_all | solution.py:91
  83.5 33.6 %all-gather.7.cloned.1.call-start = ((), (), s32[]{:S(2)}) async-start(), calls=%async_computation.6 | async-start | bytes 1310720 | tf_op jit(solution)/shard_map/all_gather | solution.py:75
  84.3 62.0 %all-reduce.7.cloned.1.call-start = ((), (), s32[]{:S(2)}) async-start(), calls=%async_computation.7 | async-start | bytes 1048576 | tf_op jit(solution)/shard_map/psum | solution.py:125
  105.9 40.4 %copy-start = (bf16[1,256,1024]{2,1,0:T(8,128)(2,1)S(1)}, bf16[1,256,1024]{2,1,0:T(8,128)(2,1)}, u32[]{:S(2)}) copy-start(bf16[1,256,1024]{2,1,0:T(8,128)(2,1)} %param.19) | copy-start | bytes 1572868
  105.9 40.4 %copy-start.15 = (f32[1024]{0:T(1024)S(1)}, f32[1024]{0:T(1024)}, u32[]{:S(2)}) copy-start(f32[1024]{0:T(1024)} %param.25) | copy-start | bytes 12292
  116.6 111.9 %copy-start.18 = (f32[1024]{0:T(1024)S(1)}, f32[1024]{0:T(1024)}, u32[]{:S(2)}) copy-start(f32[1024]{0:T(1024)} %param.26) | copy-start | bytes 12292
  116.6 111.9 %copy-start.19 = (f32[1024]{0:T(1024)S(1)}, f32[1024]{0:T(1024)}, u32[]{:S(2)}) copy-start(f32[1024]{0:T(1024)} %param.27) | copy-start | bytes 12292
  116.6 111.9 %copy-start.25 = (f32[2048]{0:T(1024)S(1)}, f32[2048]{0:T(1024)}, u32[]{:S(2)}) copy-start(f32[2048]{0:T(1024)} %param.29) | copy-start | bytes 24580
  117.1 117.0 %copy-start.8 = (bf16[1,256,4,1,128]{1,4,2,3,0:T(8,128)(2,1)}, bf16[1,256,4,1,128]{1,4,2,3,0:T(8,128)(2,1)S(1)}, u32[]{:S(2)}) copy-start(bf16[1,256,4,1,128]{1,4,2,3,0:T(8,128)(2,1)S(1)} %copy.100) | copy-start | bytes 786436
  119.7 108.7 %all-gather.9.cloned.1.call-start = ((), (), s32[]{:S(2)}) async-start(), calls=%async_computation.8 | async-start | bytes 5242880 | tf_op jit(solution)/shard_map/all_gather | solution.py:76
  120.3 188.6 %all-gather.11.cloned.1.call-start = ((), (), s32[]{:S(2)}) async-start(), calls=%async_computation.9 | async-start | bytes 5242880 | tf_op jit(solution)/shard_map/all_gather | solution.py:77
  120.9 219.7 %all-reduce.9.cloned.1.call-start = ((), (), s32[]{:S(2)}) async-start(), calls=%async_computation.10 | async-start | bytes 1048576 | tf_op jit(solution)/shard_map/psum | solution.py:135
  234.1 106.5 %copy-start.1 = (bf16[256,1024]{1,0:T(8,128)(2,1)S(1)}, bf16[256,1024]{1,0:T(8,128)(2,1)}, u32[]{:S(2)}) copy-start(bf16[256,1024]{1,0:T(8,128)(2,1)} %all-reduce.7.cloned.1.call-done) | copy-start | bytes 1572868
  234.1 106.5 %copy-start.21 = (f32[1024]{0:T(1024)S(1)}, f32[1024]{0:T(1024)}, u32[]{:S(2)}) copy-start(f32[1024]{0:T(1024)} %param.31) | copy-start | bytes 12292
  309.0 33.7 %copy-start.20 = (f32[1024]{0:T(1024)S(1)}, f32[1024]{0:T(1024)}, u32[]{:S(2)}) copy-start(f32[1024]{0:T(1024)} %param.32) | copy-start | bytes 12292
  313.6 64.9 %all-reduce.11.cloned.1.call-start = ((), (), s32[]{:S(2)}) async-start(), calls=%async_computation.11 | async-start | bytes 1048576 | tf_op jit(solution)/shard_map/psum | solution.py:149
  385.9 10.1 %all-to-all-start.2 = ((bf16[1,256,4,128]{1,3,0,2:T(8,128)(2,1)}), bf16[1,256,4,128]{1,3,0,2:T(8,128)(2,1)}, u32[]{:S(2)}, u32[]{:S(2)}) async-start(bf16[1,256,4,128]{1,3,0,2:T(8,128)(2,1)} %bitcast.233), calls=%async_computation.2 | async-start | bytes 524288 | tf_op jit(solution)/shard_map/all_to_all | solution.py:158
  412.4 18.7 %all-to-all-start.3 = ((bf16[1,1024,3,1,128]{4,2,3,0,1:T(4,128)(2,1)}), bf16[1,1024,3,1,128]{4,2,3,0,1:T(4,128)(2,1)}, u32[]{:S(2)}, u32[]{:S(2)}) async-start(bf16[1,1024,3,1,128]{4,2,3,0,1:T(4,128)(2,1)} %copy.106), calls=%async_computation.3 | async-start | bytes 2097152 | tf_op jit(solution)/shard_map/all_to_all | solution.py:216
  416.7 248.3 %reduce-scatter.2.cloned.1.call-start = ((), (), s32[]{:S(2)}) async-start(), calls=%async_computation.13 | async-start | bytes 15728640 | tf_op jit(solution)/shard_map/reduce_scatter | solution.py:245
  453.9 211.2 %copy-start.6 = (bf16[1,256,1024]{2,1,0:T(8,128)(2,1)S(1)}, bf16[1,256,1024]{2,1,0:T(8,128)(2,1)}, u32[]{:S(2)}) copy-start(bf16[1,256,1024]{2,1,0:T(8,128)(2,1)} %param.20) | copy-start | bytes 1572868
  453.9 273.7 %all-reduce.13.cloned.1.call-start = ((), (), s32[]{:S(2)}) async-start(), calls=%async_computation.12 | async-start | bytes 1048576 | tf_op jit(solution)/shard_map/psum | solution.py:232
  458.0 310.7 %all-reduce.15.cloned.1.call-start = ((), (), s32[]{:S(2)}) async-start(), calls=%async_computation.14 | async-start | bytes 6291456 | tf_op jit(solution)/shard_map/psum | solution.py:251
  (19 other events, 106.5 us)
Sparse Core Ops, SparseCore 0:
  9.6 66.1 all-gather.4
  85.9 29.0 all-gather.6
  119.9 26.3 all-reduce.6
  147.7 80.7 all-gather.8
  229.9 79.0 all-gather.10
  313.7 26.8 all-reduce.8
  349.8 28.6 all-reduce.10
  454.0 210.9 reduce-scatter.1
  667.9 29.6 all-reduce.12
  699.8 68.8 all-reduce.14
where the time goes:
time: 791 us; the launch traced here: 790 us
  waiting for transfers between devices  570 us (72%)
  blocking collectives  70.7 us (9%)
  matrix products  52.7 us (7%)
  local copies, waits for them, and re-layouts  34.8 us (4%)
  other arithmetic  33.7 us (4%)
  between operations  14.7 us (2%)
  starting transfers between devices  12.8 us (2%)
    reduce_scatter x1, waiting for transfers between devices, shards(): lax.psum_scatter(jnp.concatenate([part_qkv, part_out, part_up, part_down]...  207 us
    all_gather x1, waiting for transfers between devices, shards(): lax.all_gather(w_up, 'shard', axis=0, tiled=True)  79.5 us
    all_gather x1, waiting for transfers between devices, shards(): lax.all_gather(w_down, 'shard', axis=1, tiled=True)  74.8 us
    all_gather x1, waiting for transfers between devices, shards(): lax.all_gather(w_qkv, 'shard', axis=1, tiled=True)  66.9 us
    psum x1, blocking collectives, shards(): lax.psum((bias_qv_grad, bias_out_grad, gain_one_grad, shift_one_grad, bia...  62.3 us
    psum x1, waiting for transfers between devices, shards(): owned = lax.psum(owned.astype(jnp.bfloat16), 'ctx').astype(jnp.float32)  39.1 us
    psum x1, waiting for transfers between devices, shards(): lax.psum(back_part.astype(jnp.bfloat16), 'tp').astype(jnp.float32)  28.8 us
    psum x1, waiting for transfers between devices, shards(): lax.psum(ffn_part.astype(jnp.bfloat16), 'tp').astype(jnp.float32)  26.9 us
  transfers between devices with their start and end apart: 13, of which 11 were waited for; matrix products, arithmetic and copies ran while one was open for 5% of the time, Pallas kernels for 0%

commit v1 on v0

v1 whole, which is shorter than its diff:
```python
import math

import jax
import jax.numpy as jnp
from jax import lax
from jax.sharding import PartitionSpec as P

HEADS = 16


EPSILON = 1e-05


def normalize(resid, gain, shift):
    average = jnp.mean(resid, axis=-1, keepdims=True)
    centred = resid - average
    variance = jnp.mean(centred * centred, axis=-1, keepdims=True)
    inv_std = lax.rsqrt(variance + EPSILON)
    normed = centred * inv_std
    return (normed * gain + shift, normed, inv_std)


def normalize_back(cotan, normed, inv_std, gain):
    scaled = cotan * gain
    return inv_std * (
        scaled
        - jnp.mean(scaled, axis=-1, keepdims=True)
        - normed * jnp.mean(scaled * normed, axis=-1, keepdims=True)
    )


def gelu_value(pre_act):
    return 0.5 * pre_act * (1.0 + jax.scipy.special.erf(pre_act * 0.7071067811865476))


def gelu_slope(pre_act):
    return (
        0.5 * (1.0 + jax.scipy.special.erf(pre_act * 0.7071067811865476))
        + pre_act * jnp.exp(-0.5 * pre_act * pre_act) * 0.3989422804014327
    )


def block_scores(query_block, keys, ids_block, ids_whole, scale):
    scores = (
        jnp.einsum("qhe,khe->hqk", query_block, keys, preferred_element_type=jnp.float32) * scale
    )
    return jnp.where((ids_block[:, None] == ids_whole[None, :])[None], scores, -jnp.inf)


GROUP = ("ctx", "tp")


def dot_t(left, right):
    return lax.dot_general(
        left, right, (((1,), (1,)), ((), ())), preferred_element_type=jnp.float32
    )


def dot_rows(left, right):
    return lax.dot_general(
        left, right, (((0,), (0,)), ((), ())), preferred_element_type=jnp.float32
    )


def dot(left, right):
    return jnp.dot(left, right, preferred_element_type=jnp.float32)


def spread(part):
    return lax.all_gather(part, GROUP, axis=1, tiled=True)


def collect(whole):
    return lax.psum_scatter(whole, GROUP, scatter_dimension=1, tiled=True).astype(jnp.float32)


def shards(
    hidden_in,
    out_grad,
    segment_ids,
    w_qkv,
    bias_qv,
    w_out,
    bias_out,
    norm1_gain,
    norm1_shift,
    w_up,
    bias_up,
    w_down,
    bias_down,
    norm2_gain,
    norm2_shift,
):
    seq_count, local_len, width = hidden_in.shape
    ctx_count = lax.axis_size("ctx")
    tp_count = lax.axis_size("tp")
    ctx_at = lax.axis_index("ctx")
    tp_at = lax.axis_index("tp")
    full_len = local_len * ctx_count
    part_len = local_len // tp_count
    row_count = seq_count * full_len
    head_dim = width // HEADS
    scale = 1.0 / math.sqrt(head_dim)
    owned_rows = w_up.shape[0]
    cols = w_qkv.shape[2] // ctx_count
    units = w_up.shape[1] // ctx_count
    local_heads = cols // head_dim
    block_rows = min(512, full_len)
    block_count = full_len // block_rows

    def mine(array, size, axis):
        return lax.dynamic_slice_in_dim(array, ctx_at * size, size, axis)

    qkv_own = mine(w_qkv, cols, 2).transpose(1, 0, 2).reshape(owned_rows, 3 * cols)
    qkv_full = lax.all_gather(qkv_own, "shard", axis=0, tiled=True)
    tokens_all = lax.all_gather(hidden_in, "ctx", axis=1, tiled=True).reshape(row_count, width)
    rest_own = jnp.concatenate(
        [mine(w_out, cols, 0).T, mine(w_up, units, 1), mine(w_down, units, 0).T], axis=1
    )
    rest_full = lax.all_gather(rest_own, "shard", axis=0, tiled=True)
    out_full = rest_full[:, :cols]
    up_full = rest_full[:, cols : cols + units]
    down_full = rest_full[:, cols + units :]

    bias_own = mine(bias_qv, cols, 1)
    bias_three = jnp.concatenate([bias_own[0], jnp.zeros_like(bias_own[0]), bias_own[1]])
    project = (dot(tokens_all, qkv_full) + bias_three).astype(jnp.bfloat16)
    heads = project.reshape(seq_count, full_len, 3, local_heads, head_dim)

    def attend_sequence(packed):
        seq_heads, seq_ids = packed
        keys = seq_heads[:, 1]
        values = seq_heads[:, 2]
        queries = seq_heads[:, 0].reshape(block_count, block_rows, local_heads, head_dim)
        id_blocks = seq_ids.reshape(block_count, block_rows)

        def attend_block(piece):
            query_block, ids_block = piece
            scores = block_scores(query_block, keys, ids_block, seq_ids, scale)
            log_total = jax.nn.logsumexp(scores, axis=-1)
            probs_low = jnp.exp(scores - log_total[..., None]).astype(jnp.bfloat16)
            attended = jnp.einsum(
                "hqk,khe->qhe", probs_low, values, preferred_element_type=jnp.float32
            ).astype(jnp.bfloat16)
            return (attended, log_total)

        attended, log_total = lax.map(attend_block, (queries, id_blocks))
        return (attended.reshape(full_len, local_heads, head_dim), log_total)

    attended_heads, log_totals = lax.map(attend_sequence, (heads, segment_ids))
    attended = attended_heads.reshape(row_count, cols)

    def whole(part):
        return part.astype(jnp.bfloat16).reshape(seq_count, full_len, width)

    def part_of(array):
        return lax.dynamic_slice_in_dim(array, tp_at * part_len, part_len, 1)

    resid_one = (
        collect(whole(dot_t(attended, out_full)))
        + bias_out
        + part_of(hidden_in).astype(jnp.float32)
    )
    first, normed_one, inv_one = normalize(resid_one, norm1_gain, norm1_shift)
    first_all = spread(first.astype(jnp.bfloat16)).reshape(row_count, width)
    pre_act = dot(first_all, up_full) + mine(bias_up, units, 0)
    activated = gelu_value(pre_act).astype(jnp.bfloat16)
    resid_two = collect(whole(dot_t(activated, down_full))) + bias_down + first
    result, normed_two, inv_two = normalize(resid_two, norm2_gain, norm2_shift)
    grad_float = part_of(out_grad).astype(jnp.float32)

    def total(array):
        return jnp.sum(array, axis=(0, 1))

    gain_two_grad = total(grad_float * normed_two)
    shift_two_grad = total(grad_float)
    resid_two_grad = normalize_back(grad_float, normed_two, inv_two, norm2_gain)
    two_all = spread(resid_two_grad.astype(jnp.bfloat16)).reshape(row_count, width)
    output = lax.all_gather(result.astype(jnp.bfloat16), "tp", axis=1, tiled=True)
    bias_down_grad = total(resid_two_grad)
    pre_grad = dot(two_all, down_full) * gelu_slope(pre_act)
    pre_low = pre_grad.astype(jnp.bfloat16)
    bias_up_grad = jnp.sum(pre_grad, axis=0)
    first_grad = resid_two_grad + collect(whole(dot_t(pre_low, up_full)))
    part_ffn = jnp.concatenate(
        [dot_rows(first_all, pre_low), dot_rows(two_all, activated)], axis=1
    ).astype(jnp.bfloat16)
    gain_one_grad = total(first_grad * normed_one)
    shift_one_grad = total(first_grad)
    resid_one_grad = normalize_back(first_grad, normed_one, inv_one, norm1_gain)
    bias_out_grad = total(resid_one_grad)
    one_all = spread(resid_one_grad.astype(jnp.bfloat16)).reshape(row_count, width)
    attended_grad = dot(one_all, out_full).astype(jnp.bfloat16)
    grad_heads = attended_grad.reshape(seq_count, full_len, local_heads, head_dim)

    def back_sequence(packed):
        seq_heads, seq_ids, seq_attended, seq_grad, seq_log = packed
        keys = seq_heads[:, 1]
        values = seq_heads[:, 2]
        queries = seq_heads[:, 0].reshape(block_count, block_rows, local_heads, head_dim)
        id_blocks = seq_ids.reshape(block_count, block_rows)
        att_blocks = seq_attended.reshape(block_count, block_rows, local_heads, head_dim)
        grad_blocks = seq_grad.reshape(block_count, block_rows, local_heads, head_dim)

        def back_block(carry, piece):
            key_total, value_total = carry
            query_block, ids_block, att_block, grad_block, log_block = piece
            scores = block_scores(query_block, keys, ids_block, seq_ids, scale)
            probs = jnp.exp(scores - log_block[..., None])
            probs_low = probs.astype(jnp.bfloat16)
            prob_grad = jnp.einsum(
                "qhe,khe->hqk", grad_block, values, preferred_element_type=jnp.float32
            )
            offset = jnp.sum(
                grad_block.astype(jnp.float32) * att_block.astype(jnp.float32), axis=-1
            ).T
            score_grad = (probs * (prob_grad - offset[..., None]) * scale).astype(jnp.bfloat16)
            query_grad = jnp.einsum(
                "hqk,khe->qhe", score_grad, keys, preferred_element_type=jnp.float32
            ).astype(jnp.bfloat16)
            key_total = key_total + jnp.einsum(
                "hqk,qhe->khe", score_grad, query_block, preferred_element_type=jnp.float32
            )
            value_total = value_total + jnp.einsum(
                "hqk,qhe->khe", probs_low, grad_block, preferred_element_type=jnp.float32
            )
            return ((key_total, value_total), query_grad)

        empty = jnp.zeros((full_len, local_heads, head_dim), jnp.float32)
        (key_total, value_total), query_grads = lax.scan(
            back_block, (empty, empty), (queries, id_blocks, att_blocks, grad_blocks, seq_log)
        )
        return jnp.stack(
            [
                query_grads.reshape(full_len, local_heads, head_dim),
                key_total.astype(jnp.bfloat16),
                value_total.astype(jnp.bfloat16),
            ],
            axis=1,
        )

    head_grads = lax.map(
        back_sequence, (heads, segment_ids, attended_heads, grad_heads, log_totals)
    )
    proj_grad = head_grads.reshape(row_count, 3 * cols)
    proj_sum = jnp.sum(proj_grad.astype(jnp.float32), axis=0)
    bias_qv_grad = jnp.concatenate([proj_sum[:cols], proj_sum[2 * cols :]])
    input_part = resid_one_grad + collect(whole(dot_t(proj_grad, qkv_full)))
    input_grad = lax.all_gather(input_part.astype(jnp.bfloat16), "tp", axis=1, tiled=True)
    part_attn = jnp.concatenate(
        [dot_rows(tokens_all, proj_grad), dot_rows(one_all, attended)], axis=1
    ).astype(jnp.bfloat16)

    def owned(part):
        mean = lax.psum_scatter(part, "shard", scatter_dimension=0, tiled=True)
        return lax.all_gather(mean, "ctx", axis=0).astype(jnp.float32)

    own_ffn = owned(part_ffn)
    own_attn = owned(part_attn)
    up_grad = own_ffn[:, :, :units].transpose(1, 0, 2).reshape(w_up.shape)
    down_grad = own_ffn[:, :, units:].transpose(0, 2, 1).reshape(w_down.shape)
    qkv_grad = (
        own_attn[:, :, : 3 * cols]
        .reshape(ctx_count, owned_rows, 3, cols)
        .transpose(2, 1, 0, 3)
        .reshape(w_qkv.shape)
    )
    out_weight_grad = own_attn[:, :, 3 * cols :].transpose(0, 2, 1).reshape(w_out.shape)
    sliced = jnp.concatenate([bias_qv_grad, bias_up_grad])
    slots = jnp.zeros((tp_count, ctx_count, sliced.shape[0]), jnp.float32)
    slots = lax.dynamic_update_slice(slots, sliced[None, None], (tp_at, ctx_at, 0))
    small = lax.psum(
        jnp.concatenate(
            [
                bias_out_grad,
                gain_one_grad,
                shift_one_grad,
                bias_down_grad,
                gain_two_grad,
                shift_two_grad,
                slots.reshape(-1),
            ]
        ),
        ("shard", "ctx", "tp"),
    )
    sums = small[: 6 * width].reshape(6, width)
    slots = small[6 * width :].reshape(tp_count, ctx_count, -1)
    slots = lax.dynamic_index_in_dim(slots, tp_at, 0, keepdims=False)
    bias_qv_total = (
        slots[:, : 2 * cols].reshape(ctx_count, 2, cols).transpose(1, 0, 2).reshape(bias_qv.shape)
    )
    return (
        output,
        input_grad,
        qkv_grad,
        bias_qv_total,
        out_weight_grad,
        sums[0],
        sums[1],
        sums[2],
        up_grad,
        slots[:, 2 * cols :].reshape(bias_up.shape),
        down_grad,
        sums[3],
        sums[4],
        sums[5],
    )


def solution(mesh):
    return jax.shard_map(
        shards,
        mesh=mesh,
        in_specs=(
            P("shard", "ctx", None),
            P("shard", "ctx", None),
            P("shard", None),
            P(None, "shard", "tp"),
            P(None, "tp"),
            P("tp", "shard"),
            P(),
            P(),
            P(),
            P("shard", "tp"),
            P("tp"),
            P("tp", "shard"),
            P(),
            P(),
            P(),
        ),
        out_specs=(
            P("shard", "ctx", None),
            P("shard", "ctx", None),
            P(None, "shard", "tp"),
            P(None, "tp"),
            P("tp", "shard"),
            P(),
            P(),
            P(),
            P("shard", "tp"),
            P("tp"),
            P("tp", "shard"),
            P(),
            P(),
            P(),
        ),
        check_vma=False,
    )
```

time: 791 us -> 507 us (0.64)
  waiting for transfers between devices: 570 us -> 301 us
  other arithmetic: 33.7 us -> 20.5 us
  starting transfers between devices: 12.8 us -> 0.93 us
    psum x5 -> x0, waiting for transfers between devices: 120 us -> none  [the longest x1 39.1 us: shards(): owned = lax.psum(owned.astype(jnp.bfloat16), 'ctx').astype(jnp.float32)]
    all_gather x4 -> x7, waiting for transfers between devices: 221 us -> 126 us  [the longest x3 76.2 us: spread(): return lax.all_gather(part, GROUP, axis=1, tiled=True)]
    all_gather x0 -> x3, blocking collectives: none -> 38.4 us  [the longest x1 21.3 us: shards(): qkv_full = lax.all_gather(qkv_own, 'shard', axis=0, tiled=True)]
    reduce_scatter x1 -> x6, waiting for transfers between devices: 207 us -> 175 us  [the longest x4 132 us: collect(): lax.psum_scatter(whole, GROUP, scatter_dimension=1, tiled=True)]
    psum x1, blocking collectives: 62.3 us -> 39.6 us  [shards(): lax.psum(jnp.concatenate([bias_out_grad, gain_one_grad, shift_one_grad, b...]
    all_to_all x3 -> x0, waiting for transfers between devices: 18.9 us -> none  [the longest x1 9.59 us: shards(): lax.all_to_all(project, 'ctx', split_axis=3, concat_axis=1, tiled=True)]
    all_to_all x3 -> x0, starting transfers between devices: 12 us -> none  [the longest x1 4.25 us: shards(): lax.all_to_all(attended_grad.reshape(seq_count, local_len, ctx_count, gro...]
    transpose x2 -> x7, local copies, waits for them, and re-layouts: 2.39 us -> 13.7 us  [the longest x2 6.19 us: shards(): down_grad = own_ffn[:, :, units:].transpose(0, 2, 1).reshape(w_down.shape)]
  transfers between devices with their start and end apart: 13 -> 13, of which waited for: 11 -> 11; matrix products, arithmetic and copies ran while one was open for 5% -> 13% of each run, Pallas kernels for 0% -> 0%
where the time goes in v1:
time: 507 us; the launch traced here: 506 us
  waiting for transfers between devices  301 us (59%)
  blocking collectives  78 us (15%)
  matrix products  50.5 us (10%)
  local copies, waits for them, and re-layouts  40.4 us (8%)
  other arithmetic  20.5 us (4%)
  between operations  14.5 us (3%)
    reduce_scatter x4, waiting for transfers between devices, collect(): lax.psum_scatter(whole, GROUP, scatter_dimension=1, tiled=True)  132 us
    all_gather x3, waiting for transfers between devices, spread(): return lax.all_gather(part, GROUP, axis=1, tiled=True)  76.2 us
    reduce_scatter x2, waiting for transfers between devices, owned(): mean = lax.psum_scatter(part, 'shard', scatter_dimension=0, tiled=True)  42.8 us
    all_gather x1, waiting for transfers between devices, shards(): rest_full = lax.all_gather(rest_own, 'shard', axis=0, tiled=True)  40.8 us
    psum x1, blocking collectives, shards(): lax.psum(jnp.concatenate([bias_out_grad, gain_one_grad, shift_one_grad, b...  39.6 us
    all_gather x1, blocking collectives, shards(): qkv_full = lax.all_gather(qkv_own, 'shard', axis=0, tiled=True)  21.3 us
    dot_general x4, matrix products, dot(): return jnp.dot(left, right, preferred_element_type=jnp.float32)  14 us
    dot_general x4, matrix products, dot_t(): lax.dot_general(left, right, (((1,), (1,)), ((), ())), preferred_element_...  13.3 us
  transfers between devices with their start and end apart: 13, of which 11 were waited for; matrix products, arithmetic and copies ran while one was open for 13% of the time, Pallas kernels for 0%

profile of v1, /device:TPU:0, one launch (start us, length us, event | category | flops | bytes accessed | tf_op | source)
XLA Modules:
  0.0 506.4 jit_solution(6332370861797403989)
XLA Ops:
  14.3 21.3 %all_gather.36 = bf16[1024,384]{0,1:T(8,128)(2,1)S(1)} all-gather(bf16[256,384]{0,1:T(8,128)(2,1)S(1)} %bitcast.238), channel_id=1, replica_groups=mesh['shard'=4,'ctx'=4,'tp'=2] {'shard'}, dimensions={0}, use_global_device_ids=true | all-gather | bytes 983040 | tf_op jit(solution)/shard_map/all_gather | solution.py:115
  38.6 7.9 %while.45 = (s32[]{:T(128)}, bf16[2,512,2,64]{1,3,2,0:T(8,128)(2,1)S(1)}, f32[2,2,512]{2,1,0:T(2,128)S(1)}, s32[2,512]{1,0:T(2,128)S(1)}, s32[1024]{0:T(1024)S(1...) while((s32[]{:T(128)}, ...), condition=%wide.region_3.4_spmd, body=%wide.region_0.3_spmd.sunk | while | flops 280567808 | bytes 15526005 | solution.py:147
  46.8 40.8 %all-gather.12.cloned.1.call-done = bf16[1024,1152]{0,1:T(8,128)(2,1)} async-done(((bf16[256,1152]{0,1:T(8,128)(2,1)}), bf16[1024,1152]{0,1:T(8,128)(2,1)}) %all-gather.12.cloned.1.call-update) | async-done | bytes 2359312 | tf_op jit(solution)/shard_map/all_gather | solution.py:120
  90.8 40.0 %reduce-scatter.7.cloned.1.call-done = bf16[1,128,1024]{2,1,0:T(8,128)(2,1)} async-done(((bf16[1,1024,1024]{2,1,0:T(8,128)(2,1)}), bf16[1,128,1024]{2,1,0:T(8,128)(2,1)}) %reduce-scatter.7.cloned.1.call-update) | async-done | bytes 262160 | tf_op jit(solution)/shard_map/reduce_scatter | solution.py:74
  135.8 27.1 %all-gather.14.cloned.1.call-done = bf16[1,1024,1024]{2,1,0:T(8,128)(2,1)} async-done(((bf16[1,128,1024]{2,1,0:T(8,128)(2,1)}), bf16[1,1024,1024]{2,1,0:T(8,128)(2,1)}) %all-gather.14.cloned.1.call-update) | async-done | bytes 2097168 | tf_op jit(solution)/shard_map/all_gather | solution.py:70
  162.9 4.6 multiply_convert_fusion.1
  168.4 3.8 convert_bitcast_fusion.2
  172.3 41.2 %reduce-scatter.9.cloned.1.call-done = bf16[1,128,1024]{2,1,0:T(8,128)(2,1)} async-done(((bf16[1,1024,1024]{2,1,0:T(8,128)(2,1)}), bf16[1,128,1024]{2,1,0:T(8,128)(2,1)}) %reduce-scatter.9.cloned.1.call-update) | async-done | bytes 262160 | tf_op jit(solution)/shard_map/reduce_scatter | solution.py:74
  216.6 27.7 %all-gather.16.cloned.1.call-done = bf16[1,1024,1024]{2,1,0:T(8,128)(2,1)} async-done(((bf16[1,128,1024]{2,1,0:T(8,128)(2,1)}), bf16[1,1024,1024]{2,1,0:T(8,128)(2,1)}) %all-gather.16.cloned.1.call-update) | async-done | bytes 2097168 | tf_op jit(solution)/shard_map/all_gather | solution.py:70
  244.3 4.5 fusion.111
  249.8 3.8 convert_bitcast_fusion.1
  253.7 41.2 %reduce-scatter.11.cloned.1.call-done = bf16[1,128,1024]{2,1,0:T(8,128)(2,1)} async-done(((bf16[1,1024,1024]{2,1,0:T(8,128)(2,1)}), bf16[1,128,1024]{2,1,0:T(8,128)(2,1)}) %reduce-scatter.11.cloned.1.call-update) | async-done | bytes 262160 | tf_op jit(solution)/shard_map/reduce_scatter | solution.py:74
  299.1 3.3 fusion.72
  305.5 21.4 %all-gather.18.cloned.1.call-done = bf16[1,1024,1024]{2,1,0:T(8,128)(2,1)} async-done(((bf16[1,128,1024]{2,1,0:T(8,128)(2,1)}), bf16[1,1024,1024]{2,1,0:T(8,128)(2,1)}) %all-gather.18.cloned.1.call-update) | async-done | bytes 2097168 | tf_op jit(solution)/shard_map/all_gather | solution.py:70
  329.9 12.5 %while.46 = (s32[]{:T(128)}, f32[1024,2,64]{0,2,1:T(8,128)S(1)}, f32[1024,2,64]{0,2,1:T(8,128)}, bf16[2,512,2,64]{1,3,2,0:T(8,128)(2,1)S(1)}, bf16[2,512,2,64]{1...) while((s32[]{:T(128)}, f32[1024,2,64]{0,2,1:T(8,128)S(1)}, ...), condition=%wide.region_17.18_spmd.clone, body=%wide.region_15.17_spmd.clone.sunk | while | flops 683998208 | bytes 29526284 | solution.py:230
  348.4 25.0 %reduce-scatter.17.cloned.1.call-done = bf16[256,1024]{0,1:T(8,128)(2,1)} async-done(((bf16[1024,1024]{0,1:T(8,128)(2,1)}), bf16[256,1024]{0,1:T(8,128)(2,1)}) %reduce-scatter.17.cloned.1.call-update) | async-done | bytes 524304 | tf_op jit(solution)/shard_map/reduce_scatter | solution.py:255
  376.2 8.4 %all_gather.40 = bf16[1,256,1024]{2,1,0:T(8,128)(2,1)} all-gather(bf16[1,128,1024]{2,1,0:T(8,128)(2,1)S(1)} %get-tuple-element.297), channel_id=1, replica_groups=mesh['shard'=4,'ctx'=4,'tp'=2] {'tp'}, dimensions={1}, use_global_device_ids=true | all-gather | bytes 786432 | tf_op jit(solution)/shard_map/all_gather | solution.py:179
  385.0 17.8 %reduce-scatter.15.cloned.1.call-done = bf16[256,512]{0,1:T(8,128)(2,1)} async-done(((bf16[1024,512]{0,1:T(8,128)(2,1)}), bf16[256,512]{0,1:T(8,128)(2,1)}) %reduce-scatter.15.cloned.1.call-update) | async-done | bytes 262160 | tf_op jit(solution)/shard_map/reduce_scatter | solution.py:255
  402.8 39.6 %psum.7 = f32[12288]{0:T(1024)S(1)} all-reduce(f32[12288]{0:T(1024)S(1)} %constant_dynamic-update-slice_fusion), channel_id=1, replica_groups=mesh['shard'=4,'ctx'=4,'tp'=2] {'shard','ctx','tp'}, use_global_device_ids=true, to_apply=%region_28.29 | all-reduce | flops 12288 | bytes 98304 | tf_op jit(solution)/shard_map/psum | solution.py:272
  444.3 5.0 reshape.372
  449.3 4.5 slice_bitcast_fusion
  460.6 9.5 %reduce-scatter.13.cloned.1.call-done = bf16[1,128,1024]{2,1,0:T(8,128)(2,1)} async-done(((bf16[1,1024,1024]{2,1,0:T(8,128)(2,1)}), bf16[1,128,1024]{2,1,0:T(8,128)(2,1)}) %reduce-scatter.13.cloned.1.call-update) | async-done | bytes 262160 | tf_op jit(solution)/shard_map/reduce_scatter | solution.py:74
  471.1 8.6 %all_gather.43 = bf16[1,256,1024]{2,1,0:T(8,128)(2,1)} all-gather(bf16[1,128,1024]{2,1,0:T(8,128)(2,1)S(1)} %add_convert_fusion.1), channel_id=1, replica_groups=mesh['shard'=4,'ctx'=4,'tp'=2] {'tp'}, dimensions={1}, use_global_device_ids=true | all-gather | bytes 786432 | tf_op jit(solution)/shard_map/all_gather | solution.py:249
  479.7 8.7 %all-gather.20.cloned.1.call-done = bf16[1024,512]{0,1:T(8,128)(2,1)} async-done(((bf16[256,512]{0,1:T(8,128)(2,1)}), bf16[1024,512]{0,1:T(8,128)(2,1)}) %all-gather.20.cloned.1.call-update) | async-done | bytes 1048592 | tf_op jit(solution)/shard_map/all_gather | solution.py:256
  (213 shorter events, 83.7 us)
Async XLA Ops:
  7.2 28.5 %all-gather.10.cloned.1.call-start = ((), (), s32[]{:S(2)}) async-start(), calls=%async_computation.6 | async-start | bytes 2621440 | tf_op jit(solution)/shard_map/all_gather | solution.py:116
  7.9 79.7 %all-gather.12.cloned.1.call-start = ((), (), s32[]{:S(2)}) async-start(), calls=%async_computation.7 | async-start | bytes 2949120 | tf_op jit(solution)/shard_map/all_gather | solution.py:120
  11.3 119.5 %reduce-scatter.7.cloned.1.call-start = ((), (), s32[]{:S(2)}) async-start(), calls=%async_computation.8 | async-start | bytes 2359296 | tf_op jit(solution)/shard_map/reduce_scatter | solution.py:74
  46.5 44.2 %copy-start.13 = (bf16[1024,2,64]{0,2,1:T(8,128)(2,1)}, bf16[1024,2,64]{0,2,1:T(8,128)(2,1)S(1)}, u32[]{:S(2)}) copy-start(bf16[1024,2,64]{0,2,1:T(8,128)(2,1)S(1)} %get-tuple-element.588) | copy-start | bytes 786436
  87.6 43.2 %copy-start.3 = (bf16[1,256,1024]{2,1,0:T(8,128)(2,1)S(1)}, bf16[1,256,1024]{2,1,0:T(8,128)(2,1)}, u32[]{:S(2)}) copy-start(bf16[1,256,1024]{2,1,0:T(8,128)(2,1)} %param.19) | copy-start | bytes 1572868
  87.6 43.2 %copy-start.15 = (f32[1024]{0:T(1024)S(1)}, f32[1024]{0:T(1024)}, u32[]{:S(2)}) copy-start(f32[1024]{0:T(1024)} %param.25) | copy-start | bytes 12292
  90.7 42.4 %copy-start.16 = (f32[1024]{0:T(1024)S(1)}, f32[1024]{0:T(1024)}, u32[]{:S(2)}) copy-start(f32[1024]{0:T(1024)} %param.26) | copy-start | bytes 12292
  90.7 42.4 %copy-start.17 = (f32[1024]{0:T(1024)S(1)}, f32[1024]{0:T(1024)}, u32[]{:S(2)}) copy-start(f32[1024]{0:T(1024)} %param.27) | copy-start | bytes 12292
  90.7 72.2 %all-gather.14.cloned.1.call-start = ((), (), s32[]{:S(2)}) async-start(), calls=%async_computation.9 | async-start | bytes 2359296 | tf_op jit(solution)/shard_map/all_gather | solution.py:70
  134.9 78.6 %reduce-scatter.9.cloned.1.call-start = ((), (), s32[]{:S(2)}) async-start(), calls=%async_computation.10 | async-start | bytes 2359296 | tf_op jit(solution)/shard_map/reduce_scatter | solution.py:74
  172.2 41.3 %copy-start.2 = (bf16[1,128,1024]{2,1,0:T(8,128)(2,1)S(1)}, bf16[1,128,1024]{2,1,0:T(8,128)(2,1)}, u32[]{:S(2)}) copy-start(bf16[1,128,1024]{2,1,0:T(8,128)(2,1)} %reduce-scatter.7.cloned.1.call-done) | copy-start | bytes 786436
  172.2 41.3 %copy-start.19 = (f32[1024]{0:T(1024)S(1)}, f32[1024]{0:T(1024)}, u32[]{:S(2)}) copy-start(f32[1024]{0:T(1024)} %param.31) | copy-start | bytes 12292
  172.2 42.8 %copy-start.10 = (bf16[1,256,1024]{2,1,0:T(8,128)(2,1)S(1)}, bf16[1,256,1024]{2,1,0:T(8,128)(2,1)}, u32[]{:S(2)}) copy-start(bf16[1,256,1024]{2,1,0:T(8,128)(2,1)} %param.20) | copy-start | bytes 1572868
  172.2 42.8 %copy-start.18 = (f32[1024]{0:T(1024)S(1)}, f32[1024]{0:T(1024)}, u32[]{:S(2)}) copy-start(f32[1024]{0:T(1024)} %param.32) | copy-start | bytes 12292
  172.2 43.1 %copy-start.20 = (f32[1024]{0:T(1024)S(1)}, f32[1024]{0:T(1024)}, u32[]{:S(2)}) copy-start(f32[1024]{0:T(1024)} %param.33) | copy-start | bytes 12292
  172.3 72.0 %all-gather.16.cloned.1.call-start = ((), (), s32[]{:S(2)}) async-start(), calls=%async_computation.11 | async-start | bytes 2359296 | tf_op jit(solution)/shard_map/all_gather | solution.py:70
  216.4 78.5 %reduce-scatter.11.cloned.1.call-start = ((), (), s32[]{:S(2)}) async-start(), calls=%async_computation.12 | async-start | bytes 2359296 | tf_op jit(solution)/shard_map/reduce_scatter | solution.py:74
  253.6 73.3 %all-gather.18.cloned.1.call-start = ((), (), s32[]{:S(2)}) async-start(), calls=%async_computation.13 | async-start | bytes 2359296 | tf_op jit(solution)/shard_map/all_gather | solution.py:70
  299.0 74.5 %reduce-scatter.17.cloned.1.call-start = ((), (), s32[]{:S(2)}) async-start(), calls=%async_computation.16 | async-start | bytes 2621440 | tf_op jit(solution)/shard_map/reduce_scatter | solution.py:255
  305.3 97.5 %reduce-scatter.15.cloned.1.call-start = ((), (), s32[]{:S(2)}) async-start(), calls=%async_computation.15 | async-start | bytes 1310720 | tf_op jit(solution)/shard_map/reduce_scatter | solution.py:255
  348.4 95.9 %all-gather.22.cloned.1.call-start = ((), (), s32[]{:S(2)}) async-start(), calls=%async_computation.18 | async-start | bytes 2621440 | tf_op jit(solution)/shard_map/all_gather | solution.py:256
  373.5 96.6 %reduce-scatter.13.cloned.1.call-start = ((), (), s32[]{:S(2)}) async-start(), calls=%async_computation.14 | async-start | bytes 2359296 | tf_op jit(solution)/shard_map/reduce_scatter | solution.py:74
  376.2 112.3 %all-gather.20.cloned.1.call-start = ((), (), s32[]{:S(2)}) async-start(), calls=%async_computation.17 | async-start | bytes 1310720 | tf_op jit(solution)/shard_map/all_gather | solution.py:256
  458.4 11.7 %copy-start.5 = (f32[1,128,1024]{2,1,0:T(8,128)S(1)}, f32[1,128,1024]{2,1,0:T(8,128)}, u32[]{:S(2)}) copy-start(f32[1,128,1024]{2,1,0:T(8,128)} %copy-done.4) | copy-start | bytes 1572868
  (18 other events, 41.0 us)
Sparse Core Ops, SparseCore 0:
  9.6 25.2 all-gather.9
  37.0 50.5 all-gather.11
  91.5 39.2 reduce-scatter.6
  135.1 27.7 all-gather.13
  172.4 41.0 reduce-scatter.8
  216.5 27.7 all-gather.15
  253.7 41.0 reduce-scatter.10
  299.1 27.7 all-gather.17
  329.8 43.6 reduce-scatter.16
  376.2 26.4 reduce-scatter.14
  404.3 21.4 all-gather.21
  428.9 41.1 reduce-scatter.12
  471.6 16.7 all-gather.19

commit v2 on v1

--- a/solution.py
+++ b/solution.py
@@ -1,8 +1,11 @@
+import functools
 import math
 
 import jax
 import jax.numpy as jnp
 from jax import lax
+from jax.experimental import pallas as pl
+from jax.experimental.pallas import tpu as pltpu
 from jax.sharding import PartitionSpec as P
 
 HEADS = 16
@@ -47,9 +50,6 @@
     return jnp.where((ids_block[:, None] == ids_whole[None, :])[None], scores, -jnp.inf)
 
 
-GROUP = ("ctx", "tp")
-
-
 def dot_t(left, right):
     return lax.dot_general(
         left, right, (((1,), (1,)), ((), ())), preferred_element_type=jnp.float32
@@ -66,12 +66,160 @@
     return jnp.dot(left, right, preferred_element_type=jnp.float32)
 
 
+MESH = pl.DeviceIdType.MESH
+
+
+def places(tp_count, chip_count):
+    ctx_at = lax.axis_index("ctx")
+    tp_at = lax.axis_index("tp")
+    core = ctx_at % 2
+    chip = (ctx_at // 2) * tp_count + tp_at
+
+    def slot(at, own):
+        return ((at // tp_count) * 2 + own) * tp_count + at % tp_count
+
+    def device(at, own):
+        return {"ctx": (at // tp_count) * 2 + own, "tp": at % tp_count}
+
+    others = [(chip + step) % chip_count for step in range(chip_count)]
+    return chip, core, slot, device, others
+
+
+def greet(core, device, others):
+    barrier = pltpu.get_barrier_semaphore()
+    for step, other in enumerate(others):
+        target = device(other, core) if step else device(other, 1 - core)
+        pl.semaphore_signal(barrier, inc=1, device_id=target, device_id_type=MESH)
+    pl.semaphore_wait(barrier, len(others))
+
+
+def remote(src, dst, sems, step, target):
+    return pltpu.make_async_remote_copy(
+        src_ref=src,
+        dst_ref=dst,
+        send_sem=sems[0].at[step],
+        recv_sem=sems[1].at[step],
+        device_id=target,
+        device_id_type=MESH,
+    )
+
+
+def spread_kernel(
+    tp_count, chip_count, own_ref, all_ref, far_send, far_recv, near_send, near_recv, keep_sem
+):
+    chip, core, slot, device, others = places(tp_count, chip_count)
+    far, near = (far_send, far_recv), (near_send, near_recv)
+    greet(core, device, others)
+    mine = all_ref.at[slot(chip, core)]
+    far_copies = [
+        remote(own_ref, mine, far, step, device(others[step], core))
+        for step in range(1, chip_count)
+    ]
+    for copy in far_copies:
+        copy.start()
+    partner = device(chip, 1 - core)
+    near_copies = [remote(own_ref, mine, near, 0, partner)]
+    near_copies[0].start()
+    keep = pltpu.make_async_copy(own_ref, mine, keep_sem)
+    keep.start()
+    for step in range(1, chip_count):
+        far_copies[step - 1].wait_recv()
+        source = (chip + chip_count - step) % chip_count
+        block = all_ref.at[slot(source, core)]
+        copy = remote(block, block, near, step, partner)
+        copy.start()
+        near_copies.append(copy)
+    keep.wait()
+    for copy in far_copies:
+        copy.wait_send()
+    for copy in near_copies:
+        copy.wait()
+
+
+def collect_kernel(
+    tp_count,
+    chip_count,
+    part_ref,
+    sum_ref,
+    near_buf,
+    stage,
+    far_buf,
+    far_send,
+    far_recv,
+    near_send,
+    near_recv,
+):
+    chip, core, slot, device, others = places(tp_count, chip_count)
+    far, near = (far_send, far_recv), (near_send, near_recv)
+    greet(core, device, others)
+    partner = device(chip, 1 - core)
+    order = list(range(1, chip_count)) + [0]
+    near_copies = {}
+    for step in order:
+        block = part_ref.at[slot(others[step], 1 - core)]
+        near_copies[step] = remote(block, near_buf.at[step], near, step, partner)
+        near_copies[step].start()
+    far_copies = {}
+    for step in order:
+        near_copies[step].wait_recv()
+        both = part_ref[slot(others[step], core)].astype(jnp.float32) + near_buf[step].astype(
+            jnp.float32
+        )
+        if step:
+            stage[step] = both.astype(stage.dtype)
+            far_copies[step] = remote(
+                stage.at[step], far_buf.at[step], far, step, device(others[step], core)
+            )
+            far_copies[step].start()
+        else:
+            sum_ref[...] = both
+    for step in range(1, chip_count):
+        far_copies[step].wait_recv()
+        sum_ref[...] += far_buf[step].astype(jnp.float32)
+    for step in range(1, chip_count):
+        far_copies[step].wait_send()
+    for step in order:
+        near_copies[step].wait_send()
+
+
+def group_sizes():
+    tp_count = lax.axis_size("tp")
+    slots = lax.axis_size("ctx") * tp_count
+    return tp_count, slots, slots // 2
+
+
 def spread(part):
-    return lax.all_gather(part, GROUP, axis=1, tiled=True)
+    seq_count, part_len, width = part.shape
+    tp_count, slots, chips = group_sizes()
+    rows = seq_count * part_len
+    gathered = pl.pallas_call(
+        functools.partial(spread_kernel, tp_count, chips),
+        out_shape=jax.ShapeDtypeStruct((slots, rows, width), part.dtype),
+        in_specs=[pl.BlockSpec(memory_space=pltpu.VMEM)],
+        out_specs=pl.BlockSpec(memory_space=pltpu.VMEM),
+        scratch_shapes=[pltpu.SemaphoreType.DMA((chips,))] * 4 + [pltpu.SemaphoreType.DMA],
+        compiler_params=pltpu.CompilerParams(collective_id=0, has_side_effects=True),
+        name="spread",
+    )(part.reshape(rows, width))
+    return gathered.reshape(slots, seq_count, part_len, width).transpose(1, 0, 2, 3)
 
 
 def collect(whole):
-    return lax.psum_scatter(whole, GROUP, scatter_dimension=1, tiled=True).astype(jnp.float32)
+    seq_count, full_len, width = whole.shape
+    tp_count, slots, chips = group_sizes()
+    part_len = full_len // slots
+    rows = seq_count * part_len
+    blocks = whole.reshape(seq_count, slots, part_len, width).transpose(1, 0, 2, 3)
+    buffer = pltpu.VMEM((chips, rows, width), whole.dtype)
+    return pl.pallas_call(
+        functools.partial(collect_kernel, tp_count, chips),
+        out_shape=jax.ShapeDtypeStruct((rows, width), jnp.float32),
+        in_specs=[pl.BlockSpec(memory_space=pltpu.VMEM)],
+        out_specs=pl.BlockSpec(memory_space=pltpu.VMEM),
+        scratch_shapes=[buffer] * 3 + [pltpu.SemaphoreType.DMA((chips,))] * 4,
+        compiler_params=pltpu.CompilerParams(collective_id=1, has_side_effects=True),
+        name="collect",
+    )(blocks.reshape(slots, rows, width)).reshape(seq_count, part_len, width)
 
 
 def shards(

time: 507 us -> 439 us (0.87)
  waiting for transfers between devices: 301 us -> 105 us
  Pallas kernels: 0 us -> 132 us
    pallas_call x0 -> x7, Pallas kernels: none -> 132 us  [the longest x4 76.9 us: collect(): pl.pallas_call(functools.partial(collect_kernel, tp_count, chips), out_sh...]
    reduce_scatter x4 -> x0, waiting for transfers between devices: 132 us -> none  [collect(): lax.psum_scatter(whole, GROUP, scatter_dimension=1, tiled=True)]
    all_gather x3 -> x0, waiting for transfers between devices: 76.2 us -> none  [spread(): return lax.all_gather(part, GROUP, axis=1, tiled=True)]
    reduce_scatter x2, waiting for transfers between devices: 42.8 us -> 64 us  [owned(): mean = lax.psum_scatter(part, 'shard', scatter_dimension=0, tiled=True)]
    all_gather x2, waiting for transfers between devices: 8.73 us -> 0.01 us  [owned(): return lax.all_gather(mean, 'ctx', axis=0).astype(jnp.float32)]
  transfers between devices with their start and end apart: 13 -> 6, of which waited for: 11 -> 3; matrix products, arithmetic and copies ran while one was open for 13% -> 9% of each run, Pallas kernels for 0% -> 4%
where the time goes in v2:
time: 439 us; the launch traced here: 438 us
  Pallas kernels  132 us (30%)
  waiting for transfers between devices  105 us (24%)
  blocking collectives  79.1 us (18%)
  matrix products  50.9 us (12%)
  local copies, waits for them, and re-layouts  38.8 us (9%)
  other arithmetic  16.8 us (4%)
  between operations  14.8 us (3%)
    pallas_call x4, Pallas kernels, collect(): pl.pallas_call(functools.partial(collect_kernel, tp_count, chips), out_sh...  76.9 us
    reduce_scatter x2, waiting for transfers between devices, owned(): mean = lax.psum_scatter(part, 'shard', scatter_dimension=0, tiled=True)  64 us
    pallas_call x3, Pallas kernels, spread(): pl.pallas_call(functools.partial(spread_kernel, tp_count, chips), out_sha...  55.5 us
    psum x1, blocking collectives, shards(): lax.psum(jnp.concatenate([bias_out_grad, gain_one_grad, shift_one_grad, b...  40.2 us
    all_gather x1, waiting for transfers between devices, shards(): rest_full = lax.all_gather(rest_own, 'shard', axis=0, tiled=True)  39.7 us
    all_gather x1, blocking collectives, shards(): qkv_full = lax.all_gather(qkv_own, 'shard', axis=0, tiled=True)  21.3 us
    dot_general x4, matrix products, dot_t(): lax.dot_general(left, right, (((1,), (1,)), ((), ())), preferred_element_...  14 us
    dot_general x4, matrix products, dot(): return jnp.dot(left, right, preferred_element_type=jnp.float32)  13.6 us
  transfers between devices with their start and end apart: 6, of which 3 were waited for; matrix products, arithmetic and copies ran while one was open for 9% of the time, Pallas kernels for 4%

profile of v2, /device:TPU:0, one launch (start us, length us, event | category | flops | bytes accessed | tf_op | source)
XLA Modules:
  0.0 438.1 jit_solution(5059624007169031685)
XLA Ops:
  15.1 21.3 %all_gather.27 = bf16[1024,384]{0,1:T(8,128)(2,1)S(1)} all-gather(bf16[256,384]{0,1:T(8,128)(2,1)S(1)} %bitcast.243), channel_id=1, replica_groups=mesh['shard'=4,'ctx'=4,'tp'=2] {'shard'}, dimensions={0}, use_global_device_ids=true | all-gather | bytes 983040 | tf_op jit(solution)/shard_map/all_gather | solution.py:263
  39.6 7.9 %while.45 = (s32[]{:T(128)}, bf16[2,512,2,64]{1,3,2,0:T(8,128)(2,1)S(1)}, f32[2,2,512]{2,1,0:T(2,128)S(1)}, s32[2,512]{1,0:T(2,128)S(1)}, s32[1024]{0:T(1024)S(1...) while((s32[]{:T(128)}, ...), condition=%wide.region_3.4_spmd, body=%wide.region_0.3_spmd.sunk | while | flops 280567808 | bytes 15526005 | solution.py:295
  47.9 39.7 %all-gather.9.cloned.1.call-done = bf16[1024,1152]{0,1:T(8,128)(2,1)} async-done(((bf16[256,1152]{0,1:T(8,128)(2,1)}), bf16[1024,1152]{0,1:T(8,128)(2,1)}) %all-gather.9.cloned.1.call-update) | async-done | bytes 2359312 | tf_op jit(solution)/shard_map/all_gather | solution.py:268
  87.6 3.1 convolution_convert_fusion.4
  90.7 19.2 %collect.4 = f32[128,1024]{1,0:T(8,128)} custom-call(bf16[8,128,1024]{2,1,0:T(8,128)(2,1)} %bitcast.224), custom_call_target="tpu_custom_call" | custom-call | tf_op jit(solution)/shard_map/collect/pallas_call | solution.py:214
  112.2 18.4 %spread.3 = bf16[8,128,1024]{2,1,0:T(8,128)(2,1)} custom-call(bf16[128,1024]{1,0:T(8,128)(2,1)} %fusion.77.own_ref), custom_call_target="tpu_custom_call" | custom-call | tf_op jit(solution)/shard_map/spread/pallas_call | solution.py:195
  130.6 4.6 %multiply_convert_fusion.1 = (bf16[1024,512]{1,0:T(8,128)(2,1)S(1)}, f32[1024,512]{1,0:T(8,128)}) fusion(f32[512]{0:T(512)S(1)} %dynamic_slice.76, bf16[1024,1024]{1,0:T(8,128)(2,1)} %bitcast.233, bf16[1024,1152]{0,1:T(8,128)(2,1)} %all-gather.9.cloned.1.call-done), kind=kOutput, calls=%fused_computation.68 | convolution fusion | flops 1076887552 | bytes 6293504 | tf_op jit(solution)/shard_map/dot_general | solution.py:66
  135.2 4.2 convolution_convert_fusion.3
  139.4 19.3 %collect.5 = f32[128,1024]{1,0:T(8,128)} custom-call(bf16[8,128,1024]{2,1,0:T(8,128)(2,1)} %bitcast.231), custom_call_target="tpu_custom_call" | custom-call | tf_op jit(solution)/shard_map/collect/pallas_call | solution.py:214
  161.6 18.5 %spread.4 = bf16[8,128,1024]{2,1,0:T(8,128)(2,1)} custom-call(bf16[128,1024]{1,0:T(8,128)(2,1)} %convert_bitcast_fusion.3.own_ref), custom_call_target="tpu_custom_call" | custom-call | tf_op jit(solution)/shard_map/spread/pallas_call | solution.py:195
  180.2 4.5 %fusion.87 = (f32[512]{0:T(512)S(1)}, bf16[1024,512]{1,0:T(8,128)(2,1)S(1)}) fusion(f32[1024,512]{1,0:T(8,128)} %get-tuple-element.311, f32[512]{0:T(512)S(1)} %dynamic_slice.76, bf16[1024,1024]{1,0:T(8,128)(2,1)} %bitcast.235, bf16[1024,1152]{0,1:T(8,128)(2,1)} %all-gather.9.cloned.1.call-done), kind=kOutput, calls=%fused_computation.162 | convolution fusion | flops 1080032768 | bytes 6295552 | tf_op jit(solution)/shard_map/dot_general | solution.py:66
  184.7 4.2 convolution_convert_fusion.2
  188.9 19.2 %collect.6 = f32[128,1024]{1,0:T(8,128)} custom-call(bf16[8,128,1024]{2,1,0:T(8,128)(2,1)} %bitcast.232), custom_call_target="tpu_custom_call" | custom-call | tf_op jit(solution)/shard_map/collect/pallas_call | solution.py:214
  210.4 18.6 %spread.5 = bf16[8,128,1024]{2,1,0:T(8,128)(2,1)} custom-call(bf16[128,1024]{1,0:T(8,128)(2,1)} %convert_bitcast_fusion.2.own_ref), custom_call_target="tpu_custom_call" | custom-call | tf_op jit(solution)/shard_map/spread/pallas_call | solution.py:195
  233.6 12.5 %while.46 = (s32[]{:T(128)}, f32[1024,2,64]{0,2,1:T(8,128)S(1)}, f32[1024,2,64]{0,2,1:T(8,128)}, bf16[2,512,2,64]{1,3,2,0:T(8,128)(2,1)S(1)}, bf16[2,512,2,64]{1...) while((s32[]{:T(128)}, f32[1024,2,64]{0,2,1:T(8,128)S(1)}, ...), condition=%wide.region_14.15_spmd.clone, body=%wide.region_12.14_spmd.clone.sunk | while | flops 683998208 | bytes 29526284 | solution.py:378
  250.6 3.3 convolution_convert_fusion.5
  256.8 19.2 %reduce-scatter.3.cloned.1.call-done = bf16[256,512]{0,1:T(8,128)(2,1)} async-done(((bf16[1024,512]{0,1:T(8,128)(2,1)}), bf16[256,512]{0,1:T(8,128)(2,1)}) %reduce-scatter.3.cloned.1.call-update) | async-done | bytes 262160 | tf_op jit(solution)/shard_map/reduce_scatter | solution.py:403
  276.1 44.8 %reduce-scatter.5.cloned.1.call-done = bf16[256,1024]{0,1:T(8,128)(2,1)} async-done(((bf16[1024,1024]{0,1:T(8,128)(2,1)}), bf16[256,1024]{0,1:T(8,128)(2,1)}) %reduce-scatter.5.cloned.1.call-update) | async-done | bytes 524304 | tf_op jit(solution)/shard_map/reduce_scatter | solution.py:403
  320.9 8.4 %all_gather.30 = bf16[1,256,1024]{2,1,0:T(8,128)(2,1)} all-gather(bf16[1,128,1024]{2,1,0:T(8,128)(2,1)S(1)} %get-tuple-element.299), channel_id=1, replica_groups=mesh['shard'=4,'ctx'=4,'tp'=2] {'tp'}, dimensions={1}, use_global_device_ids=true | all-gather | bytes 786432 | tf_op jit(solution)/shard_map/all_gather | solution.py:327
  329.7 40.2 %psum.7 = f32[12288]{0:T(1024)S(1)} all-reduce(f32[12288]{0:T(1024)S(1)} %constant_dynamic-update-slice_fusion), channel_id=1, replica_groups=mesh['shard'=4,'ctx'=4,'tp'=2] {'shard','ctx','tp'}, use_global_device_ids=true, to_apply=%region_24.25 | all-reduce | flops 12288 | bytes 98304 | tf_op jit(solution)/shard_map/psum | solution.py:420
  373.8 19.2 %collect.7 = f32[128,1024]{1,0:T(8,128)} custom-call(bf16[8,128,1024]{2,1,0:T(8,128)(2,1)} %bitcast.230), custom_call_target="tpu_custom_call" | custom-call | tf_op jit(solution)/shard_map/collect/pallas_call | solution.py:214
  394.1 9.1 %all_gather.31 = bf16[1,256,1024]{2,1,0:T(8,128)(2,1)} all-gather(bf16[1,128,1024]{2,1,0:T(8,128)(2,1)S(1)} %fusion.73), channel_id=1, replica_groups=mesh['shard'=4,'ctx'=4,'tp'=2] {'tp'}, dimensions={1}, use_global_device_ids=true | all-gather | bytes 786432 | tf_op jit(solution)/shard_map/all_gather | solution.py:397
  413.5 5.0 %reshape.368 = f32[4,256,1024]{1,0,2:T(4,128)} reshape(bf16[1024,1024]{0,1:T(8,128)(2,1)} %all-gather.13.cloned.1.call-done) | data formatting | bytes 6291456 | tf_op jit(solution)/shard_map/convert_element_type | solution.py:404
  418.6 4.3 slice_bitcast_fusion
  (206 shorter events, 74.7 us)
Async XLA Ops:
  7.2 6.1 %copy-start.16 = (s32[1,1024]{1,0:T(1,128)S(1)}, s32[1,1024]{1,0:T(1,128)}, u32[]{:S(2)}) copy-start(s32[1,1024]{1,0:T(1,128)} %param.21) | copy-start | bytes 12292
  7.2 29.2 %all-gather.7.cloned.1.call-start = ((), (), s32[]{:S(2)}) async-start(), calls=%async_computation.2 | async-start | bytes 2621440 | tf_op jit(solution)/shard_map/all_gather | solution.py:264
  7.9 79.7 %all-gather.9.cloned.1.call-start = ((), (), s32[]{:S(2)}) async-start(), calls=%async_computation.3 | async-start | bytes 2949120 | tf_op jit(solution)/shard_map/all_gather | solution.py:268
  11.3 264.8 %reduce-scatter.3.cloned.1.call-start = ((), (), s32[]{:S(2)}) async-start(), calls=%async_computation.4 | async-start | bytes 1310720 | tf_op jit(solution)/shard_map/reduce_scatter | solution.py:403
  36.4 2.9 copy-start.7
  47.5 43.1 %copy-start.17 = (bf16[1024,2,64]{0,2,1:T(8,128)(2,1)}, bf16[1024,2,64]{0,2,1:T(8,128)(2,1)S(1)}, u32[]{:S(2)}) copy-start(bf16[1024,2,64]{0,2,1:T(8,128)(2,1)S(1)} %get-tuple-element.566) | copy-start | bytes 786436
  87.6 22.3 %copy-start.6 = (bf16[1,256,1024]{2,1,0:T(8,128)(2,1)S(1)}, bf16[1,256,1024]{2,1,0:T(8,128)(2,1)}, u32[]{:S(2)}) copy-start(bf16[1,256,1024]{2,1,0:T(8,128)(2,1)} %param.19) | copy-start | bytes 1572868
  87.6 22.3 %copy-start.22 = (f32[1024]{0:T(1024)S(1)}, f32[1024]{0:T(1024)}, u32[]{:S(2)}) copy-start(f32[1024]{0:T(1024)} %param.25) | copy-start | bytes 12292
  90.7 20.7 %copy-start.19 = (f32[1024]{0:T(1024)S(1)}, f32[1024]{0:T(1024)}, u32[]{:S(2)}) copy-start(f32[1024]{0:T(1024)} %param.26) | copy-start | bytes 12292
  90.7 20.7 %copy-start.20 = (f32[1024]{0:T(1024)S(1)}, f32[1024]{0:T(1024)}, u32[]{:S(2)}) copy-start(f32[1024]{0:T(1024)} %param.27) | copy-start | bytes 12292
  135.2 4.2 copy-start.26
  139.4 19.3 %copy-start.23 = (f32[1024]{0:T(1024)S(1)}, f32[1024]{0:T(1024)}, u32[]{:S(2)}) copy-start(f32[1024]{0:T(1024)} %param.31) | copy-start | bytes 12292
  139.4 20.9 %copy-start.14 = (bf16[1,256,1024]{2,1,0:T(8,128)(2,1)S(1)}, bf16[1,256,1024]{2,1,0:T(8,128)(2,1)}, u32[]{:S(2)}) copy-start(bf16[1,256,1024]{2,1,0:T(8,128)(2,1)} %param.20) | copy-start | bytes 1572868
  139.4 20.9 %copy-start.21 = (f32[1024]{0:T(1024)S(1)}, f32[1024]{0:T(1024)}, u32[]{:S(2)}) copy-start(f32[1024]{0:T(1024)} %param.32) | copy-start | bytes 12292
  184.7 4.2 copy-start.27
  250.3 70.6 %reduce-scatter.5.cloned.1.call-start = ((), (), s32[]{:S(2)}) async-start(), calls=%async_computation.5 | async-start | bytes 2621440 | tf_op jit(solution)/shard_map/reduce_scatter | solution.py:403
  250.6 3.3 copy-start.3
  250.6 3.3 copy-start.28
  256.7 114.5 %copy-start.8 = (bf16[1024,384]{0,1:T(8,128)(2,1)S(1)}, bf16[1024,384]{0,1:T(8,128)(2,1)}, u32[]{:S(2)}) copy-start(bf16[1024,384]{0,1:T(8,128)(2,1)} %copy-done.7) | copy-start | bytes 2359300
  256.7 114.5 %copy-start.10 = (bf16[1024,3,2,64]{0,3,2,1:T(8,128)(2,1)S(1)}, bf16[1024,3,2,64]{0,3,2,1:T(8,128)(2,1)}, u32[]{:S(2)}) copy-start(bf16[1024,3,2,64]{0,3,2,1:T(8,128)(2,1)} %copy-done.9) | copy-start | bytes 2359300
  256.8 147.1 %all-gather.11.cloned.1.call-start = ((), (), s32[]{:S(2)}) async-start(), calls=%async_computation.6 | async-start | bytes 1310720 | tf_op jit(solution)/shard_map/all_gather | solution.py:404
  276.1 137.5 %all-gather.13.cloned.1.call-start = ((), (), s32[]{:S(2)}) async-start(), calls=%async_computation.7 | async-start | bytes 2621440 | tf_op jit(solution)/shard_map/all_gather | solution.py:404
  427.4 3.0 copy-start.5
  427.4 3.8 copy-start.1
  (14 other events, 22.1 us)
Sparse Core Ops, SparseCore 0:
  9.6 25.2 all-gather.6
  37.0 50.5 all-gather.8
  250.4 25.5 reduce-scatter.2
  278.8 42.1 reduce-scatter.4
  322.3 16.1 all-gather.10
  340.0 23.2 all-gather.12
